TPU v7x, 256 devices: a whole 4x4x8 slice. The times are simulated.
256 devices in a mesh: sub: 64 (over x, z, core), blk: 4 (over y).
Axes of the slice: x: 4, y: 4, z: 8, core: 2. Of those that a mesh axis runs over, the one named last changes fastest.
Arguments:
- residual: float32 [64, 8, 375, 256], P('sub', 'blk'), may hold values from -6 to 6
- stiffness: bfloat16 [64, 8, 16, 375, 375], P('sub', 'blk'), may hold values from -0.078125 to 0.078125
- pattern: int32 [64, 8, 16], P('sub', 'blk'), may hold values from 0 to 7
- neumann_inv: bfloat16 [64, 8, 375, 375], P('sub', 'blk'), may hold values from -0.3125 to 0.3125
- dirichlet_inv: bfloat16 [64, 8, 375, 375], P('sub', 'blk'), may hold values from -0.3125 to 0.3125
- basis: bfloat16 [64, 8, 375, 192], P('sub', 'blk'), may hold values from -0.5 to 0.5
- node_ops: float32 [64, 6, 192, 192], P('sub'), as said below
- root_inv: float32 [192, 192], replicated, may hold values from -0.4375 to 0.4375
Outputs:
- preconditioned: float32 [64, 8, 375, 256], P('sub', 'blk')
Inputs may be any that keep to these rules, and one draw needn't show every extreme that they name: node_ops[s, l] equals node_ops[t, l] whenever s // 2**l == t // 2**l: one map for each tree node, held by all of its subdomains.
All inputs are finite; a program needn't handle non-finite values.
Results may differ from a plain program's by a relative error of at most 0.004.
Values may be sent and summed in bfloat16 or wider, within the bound.
A program may use at most 64 MiB of HBM per device.

v0:
```python
import jax
import jax.numpy as jnp
from jax import lax
from jax.sharding import PartitionSpec as P


def swapped(x, axis, distance):
    return lax.ppermute(x, axis, [(i, i ^ 1 << distance) for i in range(lax.axis_size(axis))])


def passed_along(x, axis, by):
    count = lax.axis_size(axis)
    pairs = [(i, i + by) for i in range(count) if 0 <= i + by < count]
    return lax.ppermute(x, axis, pairs)


def tree_solve(values, maps, root_inv):
    highest = lax.Precision.HIGHEST
    level_values = [values]
    current = values
    for level in range(maps.shape[0]):
        own = jnp.einsum("mk,mr->kr", maps[level], current, precision=highest)
        current = own + swapped(own, "sub", level)
        level_values.append(current)
    field = jnp.dot(root_inv, current, precision=highest)
    for level in reversed(range(maps.shape[0])):
        field = jnp.dot(maps[level], field, precision=highest) + level_values[level]
    return field


def shards(residual, stiffness, pattern, neumann_inv, dirichlet_inv, basis, node_ops, root_inv):
    subs = lax.axis_size("sub")
    here = lax.axis_index("sub")
    per_device = residual.shape[1]
    local_ids = jnp.arange(per_device)
    shared = (local_ids == 0) & (here > 0) | (local_ids == per_device - 1) & (here < subs - 1)
    scale = jnp.where(shared, 0.5, 1.0).astype(jnp.float32)[:, None, None]
    scaled_bf = (residual[0] * scale).astype(jnp.bfloat16)
    local_fix = jnp.einsum(
        "jab,jbr->jar", neumann_inv[0], scaled_bf, preferred_element_type=jnp.float32
    )
    partial_coarse = jnp.einsum(
        "jbm,jbr->mr", basis[0], scaled_bf, preferred_element_type=jnp.float32
    )
    total = lax.psum(partial_coarse, "blk")
    coarse_fix = tree_solve(total, node_ops[0], root_inv).astype(jnp.bfloat16)
    fix_term = jnp.einsum("jbm,mr->jbr", basis[0], coarse_fix, preferred_element_type=jnp.float32)
    combined = ((local_fix + fix_term) * scale)[None]
    incoming = passed_along(combined[:, -1], "sub", 1)
    first = combined[:, 0] + incoming
    returned = passed_along(first, "sub", -1)
    last = jnp.where(here < subs - 1, returned, combined[:, -1])
    assembled = jnp.concatenate([first[:, None], combined[:, 1:-1], last[:, None]], axis=1)
    assembled_bf = assembled.astype(jnp.bfloat16)
    gathered = lax.all_gather(assembled_bf, "blk", axis=1, tiled=True)
    picked = jnp.take(gathered[0], pattern[0], axis=0)
    coupled = jnp.einsum("jpab,jpbr->jar", stiffness[0], picked, preferred_element_type=jnp.float32)
    correction = jnp.einsum(
        "jab,jbr->jar",
        dirichlet_inv[0],
        coupled.astype(jnp.bfloat16),
        preferred_element_type=jnp.float32,
    )
    result = assembled[0] - jnp.where(shared[:, None, None], 0.0, correction)
    return result[None]


def solution(mesh):
    placed = (
        P("sub", "blk", None, None),
        P("sub", "blk", None, None, None),
        P("sub", "blk", None),
        P("sub", "blk", None, None),
        P("sub", "blk", None, None),
        P("sub", "blk", None, None),
        P("sub", None, None, None),
        P(),
    )
    return jax.shard_map(
        shards, mesh=mesh, in_specs=placed, out_specs=P("sub", "blk", None, None), check_vma=False
    )
```

profile of v0, /device:TPU:1, one launch (start us, length us, event | category | flops | bytes accessed | tf_op | source)
XLA Modules:
  0.0 188.2 jit_solution(13424925944676565091)
XLA Ops:
  6.6 2.3 %convolution_bitcast_fusion.14 = f32[192,256]{1,0:T(8,128)} fusion(bf16[1,2,375,192]{2,3,1,0:T(8,128)(2,1)} %param.13, f32[1,2,375,256]{3,1,2,0:T(2,128)} %param.8, f32[2]{0:T(128)S(1)} %get-tuple-element.5), kind=kOutput, calls=%fused_computation.31 | convolution fusion | flops 74112000 | bytes 1252616 | tf_op jit(solution)/shard_map/jbm,jbr->mr/dot_general | solution.py:42
  8.9 49.2 %all-reduce.2.cloned.1.call-done = f32[192,256]{1,0:T(8,128)} async-done(((f32[192,256]{1,0:T(8,128)}), f32[192,256]{1,0:T(8,128)}) %all-reduce.2.cloned.1.call-update) | async-done | bytes 196624 | tf_op jit(solution)/shard_map/psum | solution.py:45
  58.2 1.5 convolution_bitcast_fusion.13
  59.7 2.9 %collective-permute-start = (f32[192,256]{1,0:T(8,128)S(1)}, f32[192,256]{1,0:T(8,128)S(1)}, u32[]{:S(2)}, u32[]{:S(2)}) collective-permute-start(f32[192,256]{1,0:T(8,128)S(1)} %convolution_bitcast_fusion.13), channel_id=1, source_target_pairs={{0,4},{4,0},{8,12},{12,8},{16,20},{20,16},{24,28},{28,24},{32,36},... | collective-permute-start | bytes 589832 | tf_op jit(solution)/shard_map/ppermute | solution.py:8
  62.6 1.1 collective-permute-done
  63.6 0.6 convolution_bitcast_fusion.12
  64.2 1.4 collective-permute-start.1
  65.6 4.8 %collective-permute-done.1 = f32[192,256]{1,0:T(8,128)S(1)} collective-permute-done((f32[192,256]{1,0:T(8,128)S(1)}, f32[192,256]{1,0:T(8,128)S(1)}, u32[]{:S(2)}, u32[]{:S(2)}) %collective-permute-start.1) | collective-permute-done | bytes 196640 | tf_op jit(solution)/shard_map/ppermute | solution.py:8
  70.4 0.6 convolution_bitcast_fusion.11
  71.0 2.3 %collective-permute-start.2 = (f32[192,256]{1,0:T(8,128)S(1)}, f32[192,256]{1,0:T(8,128)S(1)}, u32[]{:S(2)}, u32[]{:S(2)}) collective-permute-start(f32[192,256]{1,0:T(8,128)S(1)} %convolution_bitcast_fusion.11), channel_id=1, source_target_pairs={{0,16},{4,20},{8,24},{12,28},{16,0},{20,4},{24,8},{28,12},{32,48},... | collective-permute-start | bytes 589832 | tf_op jit(solution)/shard_map/ppermute | solution.py:8
  73.4 8.7 %collective-permute-done.2 = f32[192,256]{1,0:T(8,128)S(1)} collective-permute-done((f32[192,256]{1,0:T(8,128)S(1)}, f32[192,256]{1,0:T(8,128)S(1)}, u32[]{:S(2)}, u32[]{:S(2)}) %collective-permute-start.2) | collective-permute-done | bytes 196640 | tf_op jit(solution)/shard_map/ppermute | solution.py:8
  82.1 0.6 convolution_bitcast_fusion.10
  82.7 6.4 %collective-permute-start.3 = (f32[192,256]{1,0:T(8,128)S(1)}, f32[192,256]{1,0:T(8,128)S(1)}, u32[]{:S(2)}, u32[]{:S(2)}) collective-permute-start(f32[192,256]{1,0:T(8,128)S(1)} %convolution_bitcast_fusion.10), channel_id=1, source_target_pairs={{0,32},{4,36},{8,40},{12,44},{16,48},{20,52},{24,56},{28,60},{32,0... | collective-permute-start | bytes 589832 | tf_op jit(solution)/shard_map/ppermute | solution.py:8
  89.1 7.4 %collective-permute-done.3 = f32[192,256]{1,0:T(8,128)S(1)} collective-permute-done((f32[192,256]{1,0:T(8,128)S(1)}, f32[192,256]{1,0:T(8,128)S(1)}, u32[]{:S(2)}, u32[]{:S(2)}) %collective-permute-start.3) | collective-permute-done | bytes 196640 | tf_op jit(solution)/shard_map/ppermute | solution.py:8
  96.6 0.6 convolution_bitcast_fusion.9
  97.2 1.3 collective-permute-start.4
  98.4 3.9 %collective-permute-done.4 = f32[192,256]{1,0:T(8,128)S(1)} collective-permute-done((f32[192,256]{1,0:T(8,128)S(1)}, f32[192,256]{1,0:T(8,128)S(1)}, u32[]{:S(2)}, u32[]{:S(2)}) %collective-permute-start.4) | collective-permute-done | bytes 196640 | tf_op jit(solution)/shard_map/ppermute | solution.py:8
  102.3 0.6 convolution_bitcast_fusion.8
  102.9 2.8 %collective-permute-start.5 = (f32[192,256]{1,0:T(8,128)S(1)}, f32[192,256]{1,0:T(8,128)S(1)}, u32[]{:S(2)}, u32[]{:S(2)}) collective-permute-start(f32[192,256]{1,0:T(8,128)S(1)} %convolution_bitcast_fusion.8), channel_id=1, source_target_pairs={{0,128},{4,132},{8,136},{12,140},{16,144},{20,148},{24,152},{28,15... | collective-permute-start | bytes 589832 | tf_op jit(solution)/shard_map/ppermute | solution.py:8
  105.7 3.3 %collective-permute-done.5 = f32[192,256]{1,0:T(8,128)S(1)} collective-permute-done((f32[192,256]{1,0:T(8,128)S(1)}, f32[192,256]{1,0:T(8,128)S(1)}, u32[]{:S(2)}, u32[]{:S(2)}) %collective-permute-start.5) | collective-permute-done | bytes 196640 | tf_op jit(solution)/shard_map/ppermute | solution.py:8
  112.8 2.7 %collective-permute-start.6 = (f32[1,375,256]{2,0,1:T(1,128)S(1)}, f32[1,375,256]{2,0,1:T(1,128)S(1)}, u32[]{:S(2)}, u32[]{:S(2)}) collective-permute-start(f32[1,375,256]{2,0,1:T(1,128)S(1)} %bitcast.158), channel_id=1, source_target_pairs={{0,4},{4,8},{8,12},{12,16},{16,20},{20,24},{24,28},{28,32},{32,36}... | collective-permute-start | bytes 1152008 | tf_op jit(solution)/shard_map/ppermute | solution.py:14
  115.5 4.6 %collective-permute-done.6 = f32[1,375,256]{2,0,1:T(1,128)S(1)} collective-permute-done((f32[1,375,256]{2,0,1:T(1,128)S(1)}, f32[1,375,256]{2,0,1:T(1,128)S(1)}, u32[]{:S(2)}, u32[]{:S(2)}) %collective-permute-start.6) | collective-permute-done | bytes 384032 | tf_op jit(solution)/shard_map/ppermute | solution.py:14
  120.1 0.5 fusion.36
  120.6 2.1 %collective-permute-start.7 = (f32[1,375,256]{2,0,1:T(1,128)S(1)}, f32[1,375,256]{2,0,1:T(1,128)S(1)}, u32[]{:S(2)}, u32[]{:S(2)}) collective-permute-start(f32[1,375,256]{2,0,1:T(1,128)S(1)} %fusion.36), channel_id=1, source_target_pairs={{4,0},{8,4},{12,8},{16,12},{20,16},{24,20},{28,24},{32,28},{36,32}... | collective-permute-start | bytes 1152008 | tf_op jit(solution)/shard_map/ppermute | solution.py:14
  122.7 7.6 %collective-permute-done.7 = f32[1,375,256]{2,0,1:T(1,128)S(1)} collective-permute-done((f32[1,375,256]{2,0,1:T(1,128)S(1)}, f32[1,375,256]{2,0,1:T(1,128)S(1)}, u32[]{:S(2)}, u32[]{:S(2)}) %collective-permute-start.7) | collective-permute-done | bytes 384032 | tf_op jit(solution)/shard_map/ppermute | solution.py:14
  130.3 0.5 fusion.35
  130.8 0.7 fusion.39
  131.6 0.8 copy.30
  132.5 31.0 %all-gather.2.cloned.1.call-done = bf16[1,8,375,256]{3,2,0,1:T(8,128)(2,1)} async-done(((bf16[1,2,375,256]{3,2,0,1:T(8,128)(2,1)}), bf16[1,8,375,256]{3,2,0,1:T(8,128)(2,1)}) %all-gather.2.cloned.1.call-update) | async-done | bytes 1536016 | tf_op jit(solution)/shard_map/all_gather | solution.py:55
  163.5 5.0 %gather_fusion = bf16[32,375,256]{2,1,0:T(8,128)(2,1)} fusion(bf16[8,375,256]{2,1,0:T(8,128)(2,1)} %bitcast.154, s32[1024]{0:T(1024)S(1)} %pad_clamp_fusion), kind=kCustom, calls=%fused_computation | custom fusion | bytes 12288128 | tf_op jit(solution)/shard_map/jit(_take)/gather | solution.py:56
  168.5 11.0 %fusion.28 = f32[2,256,375]{1,2,0:T(8,128)S(1)} fusion(bf16[2,375,375]{2,0,1:T(2,128)(2,1)S(1)} %bitcast.160, bf16[2,16,375,375]{3,1,2,0:T(8,128)(2,1)} %bitcast.159, bf16[2,16,375,256]{3,2,1,0:T(8,128)(2,1)} %bitcast.155, pred[2,16]{1,0:T(4,128)(4,1)S(1)} %compare_and_fusion), kind=kOutput, calls=%fused_computation.41 | convolution fusion | flops 2451264000 | bytes 16474532 | tf_op jit(solution)/shard_map/jab,jbr->jar/dot_general | solution.py:58
  179.6 1.8 fusion.27
  (41 shorter events, 4.0 us)
Async XLA Ops:
  6.5 105.2 %copy-start = (bf16[1,2,375,375]{3,1,2,0:T(2,128)(2,1)S(1)}, bf16[1,2,375,375]{3,1,2,0:T(2,128)(2,1)}, u32[]{:S(2)}) copy-start(bf16[1,2,375,375]{3,1,2,0:T(2,128)(2,1)} %param.11) | copy-start | bytes 1687504
  6.5 51.6 %copy-start.1 = (f32[1,6,192,192]{3,2,1,0:T(8,128)S(1)}, f32[1,6,192,192]{3,2,1,0:T(8,128)}, u32[]{:S(2)}) copy-start(f32[1,6,192,192]{3,2,1,0:T(8,128)} %param.14) | copy-start | bytes 2654212
  6.5 51.6 %all-reduce.2.cloned.1.call-start = ((), (), s32[]{:S(2)}) async-start(), calls=%async_computation | async-start | bytes 393216 | tf_op jit(solution)/shard_map/psum | solution.py:45
  8.9 154.6 %all-gather.2.cloned.1.call-start = ((), (), s32[]{:S(2)}) async-start(), calls=%async_computation.1 | async-start | bytes 1925120 | tf_op jit(solution)/shard_map/all_gather | solution.py:55
  59.7 3.9 %collective-permute-start = (f32[192,256]{1,0:T(8,128)S(1)}, f32[192,256]{1,0:T(8,128)S(1)}, u32[]{:S(2)}, u32[]{:S(2)}) collective-permute-start(f32[192,256]{1,0:T(8,128)S(1)} %convolution_bitcast_fusion.13), channel_id=1, source_target_pairs={{0,4},{4,0},{8,12},{12,8},{16,20},{20,16},{24,28},{28,24},{32,36},... | collective-permute-start | bytes 589832 | tf_op jit(solution)/shard_map/ppermute | solution.py:8
  64.2 6.2 %collective-permute-start.1 = (f32[192,256]{1,0:T(8,128)S(1)}, f32[192,256]{1,0:T(8,128)S(1)}, u32[]{:S(2)}, u32[]{:S(2)}) collective-permute-start(f32[192,256]{1,0:T(8,128)S(1)} %convolution_bitcast_fusion.12), channel_id=1, source_target_pairs={{0,8},{4,12},{8,0},{12,4},{16,24},{20,28},{24,16},{28,20},{32,40},... | collective-permute-start | bytes 589832 | tf_op jit(solution)/shard_map/ppermute | solution.py:8
  71.0 11.0 %collective-permute-start.2 = (f32[192,256]{1,0:T(8,128)S(1)}, f32[192,256]{1,0:T(8,128)S(1)}, u32[]{:S(2)}, u32[]{:S(2)}) collective-permute-start(f32[192,256]{1,0:T(8,128)S(1)} %convolution_bitcast_fusion.11), channel_id=1, source_target_pairs={{0,16},{4,20},{8,24},{12,28},{16,0},{20,4},{24,8},{28,12},{32,48},... | collective-permute-start | bytes 589832 | tf_op jit(solution)/shard_map/ppermute | solution.py:8
  82.7 26.4 %copy-start.5 = (f32[192,192]{1,0:T(8,128)S(1)}, f32[192,192]{1,0:T(8,128)}, u32[]{:S(2)}) copy-start(f32[192,192]{1,0:T(8,128)} %param.15) | copy-start | bytes 442372
  82.7 13.9 %collective-permute-start.3 = (f32[192,256]{1,0:T(8,128)S(1)}, f32[192,256]{1,0:T(8,128)S(1)}, u32[]{:S(2)}, u32[]{:S(2)}) collective-permute-start(f32[192,256]{1,0:T(8,128)S(1)} %convolution_bitcast_fusion.10), channel_id=1, source_target_pairs={{0,32},{4,36},{8,40},{12,44},{16,48},{20,52},{24,56},{28,60},{32,0... | collective-permute-start | bytes 589832 | tf_op jit(solution)/shard_map/ppermute | solution.py:8
  97.2 5.1 %collective-permute-start.4 = (f32[192,256]{1,0:T(8,128)S(1)}, f32[192,256]{1,0:T(8,128)S(1)}, u32[]{:S(2)}, u32[]{:S(2)}) collective-permute-start(f32[192,256]{1,0:T(8,128)S(1)} %convolution_bitcast_fusion.9), channel_id=1, source_target_pairs={{0,64},{4,68},{8,72},{12,76},{16,80},{20,84},{24,88},{28,92},{32,9... | collective-permute-start | bytes 589832 | tf_op jit(solution)/shard_map/ppermute | solution.py:8
  102.9 6.1 %collective-permute-start.5 = (f32[192,256]{1,0:T(8,128)S(1)}, f32[192,256]{1,0:T(8,128)S(1)}, u32[]{:S(2)}, u32[]{:S(2)}) collective-permute-start(f32[192,256]{1,0:T(8,128)S(1)} %convolution_bitcast_fusion.8), channel_id=1, source_target_pairs={{0,128},{4,132},{8,136},{12,140},{16,144},{20,148},{24,152},{28,15... | collective-permute-start | bytes 589832 | tf_op jit(solution)/shard_map/ppermute | solution.py:8
  110.0 1.0 copy-start.4
  110.4 1.0 copy-start.3
  110.7 1.1 copy-start.2
  112.8 7.3 %collective-permute-start.6 = (f32[1,375,256]{2,0,1:T(1,128)S(1)}, f32[1,375,256]{2,0,1:T(1,128)S(1)}, u32[]{:S(2)}, u32[]{:S(2)}) collective-permute-start(f32[1,375,256]{2,0,1:T(1,128)S(1)} %bitcast.158), channel_id=1, source_target_pairs={{0,4},{4,8},{8,12},{12,16},{16,20},{20,24},{24,28},{28,32},{32,36}... | collective-permute-start | bytes 1152008 | tf_op jit(solution)/shard_map/ppermute | solution.py:14
  120.6 9.7 %collective-permute-start.7 = (f32[1,375,256]{2,0,1:T(1,128)S(1)}, f32[1,375,256]{2,0,1:T(1,128)S(1)}, u32[]{:S(2)}, u32[]{:S(2)}) collective-permute-start(f32[1,375,256]{2,0,1:T(1,128)S(1)} %fusion.36), channel_id=1, source_target_pairs={{4,0},{8,4},{12,8},{16,12},{20,16},{24,20},{28,24},{32,28},{36,32}... | collective-permute-start | bytes 1152008 | tf_op jit(solution)/shard_map/ppermute | solution.py:14
  130.8 1.5 copy-start.6
  163.5 5.0 %copy-start.7 = (bf16[1,2,375,375]{3,1,2,0:T(2,128)(2,1)S(1)}, bf16[1,2,375,375]{3,1,2,0:T(2,128)(2,1)}, u32[]{:S(2)}) copy-start(bf16[1,2,375,375]{3,1,2,0:T(2,128)(2,1)} %param.12) | copy-start | bytes 1687504
Sparse Core Ops, SparseCore 0:
  9.7 48.4 all-reduce.1
  132.5 30.9 all-gather.1
where the time goes:
time: 188 us
  waiting for transfers between devices  122 us (65%)
  starting transfers between devices  21.9 us (12%)
  matrix products  20.8 us (11%)
  between operations  13.6 us (7%)
  local copies, waits for them, and re-layouts  6.44 us (3%)
  other arithmetic  3.71 us (2%)
    psum x1, waiting for transfers between devices, shards(): total = lax.psum(partial_coarse, 'blk')  49.2 us
    all_gather x1, waiting for transfers between devices, shards(): gathered = lax.all_gather(assembled_bf, 'blk', axis=1, tiled=True)  31 us
    ppermute x6, waiting for transfers between devices, swapped(): lax.ppermute(x, axis, [(i, i ^ 1 << distance) for i in range(lax.axis_siz...  29.2 us
    ppermute x6, starting transfers between devices, swapped(): lax.ppermute(x, axis, [(i, i ^ 1 << distance) for i in range(lax.axis_siz...  17.1 us
    ppermute x2, waiting for transfers between devices, passed_along(): return lax.ppermute(x, axis, pairs)  12.2 us
    dot_general x1, matrix products, shards(): jnp.einsum('jab,jbr->jar', dirichlet_inv[0], coupled.astype(jnp.bfloat16)...  11 us
    gather x1, local copies, waits for them, and re-layouts, shards(): picked = jnp.take(gathered[0], pattern[0], axis=0)  5.01 us
    ppermute x2, starting transfers between devices, passed_along(): return lax.ppermute(x, axis, pairs)  4.79 us
  transfers between devices with their start and end apart: 10, of which 10 were waited for; matrix products, arithmetic and copies ran while one was open for 0% of the time, Pallas kernels for 0%

commit v1 on v0

--- a/solution.py
+++ b/solution.py
@@ -42,7 +42,7 @@
     partial_coarse = jnp.einsum(
         "jbm,jbr->mr", basis[0], scaled_bf, preferred_element_type=jnp.float32
     )
-    total = lax.psum(partial_coarse, "blk")
+    total = jnp.sum(lax.all_gather(partial_coarse, "blk"), axis=0)
     coarse_fix = tree_solve(total, node_ops[0], root_inv).astype(jnp.bfloat16)
     fix_term = jnp.einsum("jbm,mr->jbr", basis[0], coarse_fix, preferred_element_type=jnp.float32)
     combined = ((local_fix + fix_term) * scale)[None]

time: 188 us -> 153 us (0.81)
  waiting for transfers between devices: 122 us -> 81.9 us
  blocking collectives: 0 us -> 13.3 us
  starting transfers between devices: 21.9 us -> 14.7 us
    psum x1 -> x0, waiting for transfers between devices: 49.2 us -> none  [shards(): total = lax.psum(partial_coarse, 'blk')]
    all_gather x0 -> x1, blocking collectives: none -> 13.3 us  [shards(): total = jnp.sum(lax.all_gather(partial_coarse, 'blk'), axis=0)]
    ppermute x6, waiting for transfers between devices: 29.2 us -> 38.2 us  [swapped(): lax.ppermute(x, axis, [(i, i ^ 1 << distance) for i in range(lax.axis_siz...]
    ppermute x6, starting transfers between devices: 17.1 us -> 10.6 us  [swapped(): lax.ppermute(x, axis, [(i, i ^ 1 << distance) for i in range(lax.axis_siz...]
  transfers between devices with their start and end apart: 10 -> 9, of which waited for: 10 -> 9; matrix products, arithmetic and copies ran while one was open for 0% -> 0% of each run, Pallas kernels for 0% -> 0%
where the time goes in v1:
time: 153 us
  waiting for transfers between devices  81.9 us (54%)
  matrix products  19.1 us (12%)
  starting transfers between devices  14.7 us (10%)
  between operations  13.7 us (9%)
  blocking collectives  13.3 us (9%)
  local copies, waits for them, and re-layouts  6.47 us (4%)
  other arithmetic  3.76 us (2%)
    ppermute x6, waiting for transfers between devices, swapped(): lax.ppermute(x, axis, [(i, i ^ 1 << distance) for i in range(lax.axis_siz...  38.2 us
    all_gather x1, waiting for transfers between devices, shards(): gathered = lax.all_gather(assembled_bf, 'blk', axis=1, tiled=True)  31.5 us
    all_gather x1, blocking collectives, shards(): total = jnp.sum(lax.all_gather(partial_coarse, 'blk'), axis=0)  13.3 us
    ppermute x2, waiting for transfers between devices, passed_along(): return lax.ppermute(x, axis, pairs)  12.2 us
    dot_general x1, matrix products, shards(): jnp.einsum('jab,jbr->jar', dirichlet_inv[0], coupled.astype(jnp.bfloat16)...  11 us
    ppermute x6, starting transfers between devices, swapped(): lax.ppermute(x, axis, [(i, i ^ 1 << distance) for i in range(lax.axis_siz...  10.6 us
    gather x1, local copies, waits for them, and re-layouts, shards(): picked = jnp.take(gathered[0], pattern[0], axis=0)  5.03 us
    ppermute x2, starting transfers between devices, passed_along(): return lax.ppermute(x, axis, pairs)  4.02 us
  transfers between devices with their start and end apart: 9, of which 9 were waited for; matrix products, arithmetic and copies ran while one was open for 0% of the time, Pallas kernels for 0%

profile of v1, /device:TPU:1, one launch (start us, length us, event | category | flops | bytes accessed | tf_op | source)
XLA Modules:
  0.0 153.0 jit_solution(7815360209997608733)
XLA Ops:
  6.5 1.6 %convolution_bitcast_fusion.14 = f32[192,256]{1,0:T(8,128)S(1)} fusion(bf16[1,2,375,192]{2,3,1,0:T(8,128)(2,1)} %param.13, f32[1,2,375,256]{3,1,2,0:T(2,128)} %param.8, f32[2]{0:T(128)S(1)} %get-tuple-element.5), kind=kOutput, calls=%fused_computation.31 | convolution fusion | flops 74112000 | bytes 1252616 | tf_op jit(solution)/shard_map/jbm,jbr->mr/dot_general | solution.py:42
  8.1 13.3 %all-gather = f32[768,256]{1,0:T(8,128)S(1)} all-gather(f32[192,256]{1,0:T(8,128)S(1)} %convolution_bitcast_fusion.14), channel_id=2, replica_groups=mesh['sub'=64,'blk'=4] {'blk'}, dimensions={0}, use_global_device_ids=true | all-gather | bytes 983040 | tf_op jit(solution)/shard_map/all_gather | solution.py:45
  21.5 0.6 convolution_bitcast_fusion.13
  22.1 4.2 %collective-permute-start = (f32[192,256]{1,0:T(8,128)S(1)}, f32[192,256]{1,0:T(8,128)S(1)}, u32[]{:S(2)}, u32[]{:S(2)}) collective-permute-start(f32[192,256]{1,0:T(8,128)S(1)} %convolution_bitcast_fusion.13), channel_id=1, source_target_pairs={{0,4},{4,0},{8,12},{12,8},{16,20},{20,16},{24,28},{28,24},{32,36},... | collective-permute-start | bytes 589832 | tf_op jit(solution)/shard_map/ppermute | solution.py:8
  26.3 1.1 collective-permute-done
  27.4 0.6 convolution_bitcast_fusion.12
  28.1 6.1 %collective-permute-done.1 = f32[192,256]{1,0:T(8,128)S(1)} collective-permute-done((f32[192,256]{1,0:T(8,128)S(1)}, f32[192,256]{1,0:T(8,128)S(1)}, u32[]{:S(2)}, u32[]{:S(2)}) %collective-permute-start.1) | collective-permute-done | bytes 196640 | tf_op jit(solution)/shard_map/ppermute | solution.py:8
  34.2 0.6 convolution_bitcast_fusion.11
  34.8 1.4 collective-permute-start.2
  36.2 10.6 %collective-permute-done.2 = f32[192,256]{1,0:T(8,128)S(1)} collective-permute-done((f32[192,256]{1,0:T(8,128)S(1)}, f32[192,256]{1,0:T(8,128)S(1)}, u32[]{:S(2)}, u32[]{:S(2)}) %collective-permute-start.2) | collective-permute-done | bytes 196640 | tf_op jit(solution)/shard_map/ppermute | solution.py:8
  46.8 0.6 convolution_bitcast_fusion.10
  47.4 4.6 %collective-permute-start.3 = (f32[192,256]{1,0:T(8,128)S(1)}, f32[192,256]{1,0:T(8,128)S(1)}, u32[]{:S(2)}, u32[]{:S(2)}) collective-permute-start(f32[192,256]{1,0:T(8,128)S(1)} %convolution_bitcast_fusion.10), channel_id=1, source_target_pairs={{0,32},{4,36},{8,40},{12,44},{16,48},{20,52},{24,56},{28,60},{32,0... | collective-permute-start | bytes 589832 | tf_op jit(solution)/shard_map/ppermute | solution.py:8
  52.0 9.6 %collective-permute-done.3 = f32[192,256]{1,0:T(8,128)S(1)} collective-permute-done((f32[192,256]{1,0:T(8,128)S(1)}, f32[192,256]{1,0:T(8,128)S(1)}, u32[]{:S(2)}, u32[]{:S(2)}) %collective-permute-start.3) | collective-permute-done | bytes 196640 | tf_op jit(solution)/shard_map/ppermute | solution.py:8
  61.6 0.6 convolution_bitcast_fusion.9
  62.3 5.0 %collective-permute-done.4 = f32[192,256]{1,0:T(8,128)S(1)} collective-permute-done((f32[192,256]{1,0:T(8,128)S(1)}, f32[192,256]{1,0:T(8,128)S(1)}, u32[]{:S(2)}, u32[]{:S(2)}) %collective-permute-start.4) | collective-permute-done | bytes 196640 | tf_op jit(solution)/shard_map/ppermute | solution.py:8
  67.4 0.6 convolution_bitcast_fusion.8
  68.2 5.8 %collective-permute-done.5 = f32[192,256]{1,0:T(8,128)S(1)} collective-permute-done((f32[192,256]{1,0:T(8,128)S(1)}, f32[192,256]{1,0:T(8,128)S(1)}, u32[]{:S(2)}, u32[]{:S(2)}) %collective-permute-start.5) | collective-permute-done | bytes 196640 | tf_op jit(solution)/shard_map/ppermute | solution.py:8
  74.1 0.3 fusion.52
  76.9 0.4 fusion.12
  77.4 0.4 copy.61
  77.8 1.9 %collective-permute-start.6 = (f32[1,375,256]{2,0,1:T(1,128)S(1)}, f32[1,375,256]{2,0,1:T(1,128)S(1)}, u32[]{:S(2)}, u32[]{:S(2)}) collective-permute-start(f32[1,375,256]{2,0,1:T(1,128)S(1)} %bitcast.160), channel_id=1, source_target_pairs={{0,4},{4,8},{8,12},{12,16},{16,20},{20,24},{24,28},{28,32},{32,36}... | collective-permute-start | bytes 1152008 | tf_op jit(solution)/shard_map/ppermute | solution.py:14
  79.7 4.6 %collective-permute-done.6 = f32[1,375,256]{2,0,1:T(1,128)S(1)} collective-permute-done((f32[1,375,256]{2,0,1:T(1,128)S(1)}, f32[1,375,256]{2,0,1:T(1,128)S(1)}, u32[]{:S(2)}, u32[]{:S(2)}) %collective-permute-start.6) | collective-permute-done | bytes 384032 | tf_op jit(solution)/shard_map/ppermute | solution.py:14
  84.3 0.5 fusion.36
  84.9 2.1 %collective-permute-start.7 = (f32[1,375,256]{2,0,1:T(1,128)S(1)}, f32[1,375,256]{2,0,1:T(1,128)S(1)}, u32[]{:S(2)}, u32[]{:S(2)}) collective-permute-start(f32[1,375,256]{2,0,1:T(1,128)S(1)} %fusion.36), channel_id=1, source_target_pairs={{4,0},{8,4},{12,8},{16,12},{20,16},{24,20},{28,24},{32,28},{36,32}... | collective-permute-start | bytes 1152008 | tf_op jit(solution)/shard_map/ppermute | solution.py:14
  87.0 7.6 %collective-permute-done.7 = f32[1,375,256]{2,0,1:T(1,128)S(1)} collective-permute-done((f32[1,375,256]{2,0,1:T(1,128)S(1)}, f32[1,375,256]{2,0,1:T(1,128)S(1)}, u32[]{:S(2)}, u32[]{:S(2)}) %collective-permute-start.7) | collective-permute-done | bytes 384032 | tf_op jit(solution)/shard_map/ppermute | solution.py:14
  94.6 0.5 fusion.35
  95.1 0.7 fusion.39
  95.8 0.8 copy.30
  96.8 31.5 %all-gather.3.cloned.1.call-done = bf16[1,8,375,256]{3,2,0,1:T(8,128)(2,1)} async-done(((bf16[1,2,375,256]{3,2,0,1:T(8,128)(2,1)}), bf16[1,8,375,256]{3,2,0,1:T(8,128)(2,1)}) %all-gather.3.cloned.1.call-update) | async-done | bytes 1536016 | tf_op jit(solution)/shard_map/all_gather | solution.py:55
  128.2 5.0 %gather_fusion = bf16[32,375,256]{2,1,0:T(8,128)(2,1)} fusion(bf16[8,375,256]{2,1,0:T(8,128)(2,1)} %bitcast.155, s32[1024]{0:T(1024)S(1)} %pad_clamp_fusion), kind=kCustom, calls=%fused_computation | custom fusion | bytes 12288128 | tf_op jit(solution)/shard_map/jit(_take)/gather | solution.py:56
  133.2 11.0 %fusion.28 = f32[2,256,375]{1,2,0:T(8,128)S(1)} fusion(bf16[2,375,375]{2,0,1:T(2,128)(2,1)S(1)} %bitcast.162, bf16[2,16,375,375]{3,1,2,0:T(8,128)(2,1)} %bitcast.161, bf16[2,16,375,256]{3,2,1,0:T(8,128)(2,1)} %bitcast.156, pred[2,16]{1,0:T(4,128)(4,1)S(1)} %compare_and_fusion), kind=kOutput, calls=%fused_computation.41 | convolution fusion | flops 2451264000 | bytes 16474532 | tf_op jit(solution)/shard_map/jab,jbr->jar/dot_general | solution.py:58
  144.3 1.8 %fusion.27 = f32[1,2,375,256]{3,1,2,0:T(2,128)} fusion(f32[2,256,375]{1,2,0:T(8,128)S(1)} %fusion.28, pred[2]{0:T(512)(128)(4,1)S(1)} %get-tuple-element.6, f32[1,1,375,256]{3,1,2,0:T(1,128)S(1)} %fusion.35, f32[1,1,375,256]{3,1,2,0:T(1,128)S(1)} %bitcast.158), kind=kLoop, calls=%fused_computation.38 | loop fusion | flops 576000 | bytes 2304002 | tf_op jit(solution)/shard_map/broadcast_in_dim | solution.py:65
  (38 shorter events, 3.3 us)
Async XLA Ops:
  6.5 70.3 %copy-start = (bf16[1,2,375,375]{3,1,2,0:T(2,128)(2,1)S(1)}, bf16[1,2,375,375]{3,1,2,0:T(2,128)(2,1)}, u32[]{:S(2)}) copy-start(bf16[1,2,375,375]{3,1,2,0:T(2,128)(2,1)} %param.11) | copy-start | bytes 1687504
  6.5 121.7 %all-gather.3.cloned.1.call-start = ((), (), s32[]{:S(2)}) async-start(), calls=%async_computation | async-start | bytes 1925120 | tf_op jit(solution)/shard_map/all_gather | solution.py:55
  8.1 13.4 %copy-start.1 = (f32[1,6,192,192]{3,2,1,0:T(8,128)S(1)}, f32[1,6,192,192]{3,2,1,0:T(8,128)}, u32[]{:S(2)}) copy-start(f32[1,6,192,192]{3,2,1,0:T(8,128)} %param.14) | copy-start | bytes 2654212
  22.1 5.3 %collective-permute-start = (f32[192,256]{1,0:T(8,128)S(1)}, f32[192,256]{1,0:T(8,128)S(1)}, u32[]{:S(2)}, u32[]{:S(2)}) collective-permute-start(f32[192,256]{1,0:T(8,128)S(1)} %convolution_bitcast_fusion.13), channel_id=1, source_target_pairs={{0,4},{4,0},{8,12},{12,8},{16,20},{20,16},{24,28},{28,24},{32,36},... | collective-permute-start | bytes 589832 | tf_op jit(solution)/shard_map/ppermute | solution.py:8
  28.0 6.2 %collective-permute-start.1 = (f32[192,256]{1,0:T(8,128)S(1)}, f32[192,256]{1,0:T(8,128)S(1)}, u32[]{:S(2)}, u32[]{:S(2)}) collective-permute-start(f32[192,256]{1,0:T(8,128)S(1)} %convolution_bitcast_fusion.12), channel_id=1, source_target_pairs={{0,8},{4,12},{8,0},{12,4},{16,24},{20,28},{24,16},{28,20},{32,40},... | collective-permute-start | bytes 589832 | tf_op jit(solution)/shard_map/ppermute | solution.py:8
  34.8 12.0 %collective-permute-start.2 = (f32[192,256]{1,0:T(8,128)S(1)}, f32[192,256]{1,0:T(8,128)S(1)}, u32[]{:S(2)}, u32[]{:S(2)}) collective-permute-start(f32[192,256]{1,0:T(8,128)S(1)} %convolution_bitcast_fusion.11), channel_id=1, source_target_pairs={{0,16},{4,20},{8,24},{12,28},{16,0},{20,4},{24,8},{28,12},{32,48},... | collective-permute-start | bytes 589832 | tf_op jit(solution)/shard_map/ppermute | solution.py:8
  47.4 26.6 %copy-start.4 = (f32[192,192]{1,0:T(8,128)S(1)}, f32[192,192]{1,0:T(8,128)}, u32[]{:S(2)}) copy-start(f32[192,192]{1,0:T(8,128)} %param.15) | copy-start | bytes 442372
  47.4 14.2 %collective-permute-start.3 = (f32[192,256]{1,0:T(8,128)S(1)}, f32[192,256]{1,0:T(8,128)S(1)}, u32[]{:S(2)}, u32[]{:S(2)}) collective-permute-start(f32[192,256]{1,0:T(8,128)S(1)} %convolution_bitcast_fusion.10), channel_id=1, source_target_pairs={{0,32},{4,36},{8,40},{12,44},{16,48},{20,52},{24,56},{28,60},{32,0... | collective-permute-start | bytes 589832 | tf_op jit(solution)/shard_map/ppermute | solution.py:8
  62.2 5.1 %collective-permute-start.4 = (f32[192,256]{1,0:T(8,128)S(1)}, f32[192,256]{1,0:T(8,128)S(1)}, u32[]{:S(2)}, u32[]{:S(2)}) collective-permute-start(f32[192,256]{1,0:T(8,128)S(1)} %convolution_bitcast_fusion.9), channel_id=1, source_target_pairs={{0,64},{4,68},{8,72},{12,76},{16,80},{20,84},{24,88},{28,92},{32,9... | collective-permute-start | bytes 589832 | tf_op jit(solution)/shard_map/ppermute | solution.py:8
  68.0 6.1 %collective-permute-start.5 = (f32[192,256]{1,0:T(8,128)S(1)}, f32[192,256]{1,0:T(8,128)S(1)}, u32[]{:S(2)}, u32[]{:S(2)}) collective-permute-start(f32[192,256]{1,0:T(8,128)S(1)} %convolution_bitcast_fusion.8), channel_id=1, source_target_pairs={{0,128},{4,132},{8,136},{12,140},{16,144},{20,148},{24,152},{28,15... | collective-permute-start | bytes 589832 | tf_op jit(solution)/shard_map/ppermute | solution.py:8
  75.4 1.0 copy-start.3
  75.8 1.1 copy-start.2
  77.8 6.5 %collective-permute-start.6 = (f32[1,375,256]{2,0,1:T(1,128)S(1)}, f32[1,375,256]{2,0,1:T(1,128)S(1)}, u32[]{:S(2)}, u32[]{:S(2)}) collective-permute-start(f32[1,375,256]{2,0,1:T(1,128)S(1)} %bitcast.160), channel_id=1, source_target_pairs={{0,4},{4,8},{8,12},{12,16},{16,20},{20,24},{24,28},{28,32},{32,36}... | collective-permute-start | bytes 1152008 | tf_op jit(solution)/shard_map/ppermute | solution.py:14
  84.9 9.7 %collective-permute-start.7 = (f32[1,375,256]{2,0,1:T(1,128)S(1)}, f32[1,375,256]{2,0,1:T(1,128)S(1)}, u32[]{:S(2)}, u32[]{:S(2)}) collective-permute-start(f32[1,375,256]{2,0,1:T(1,128)S(1)} %fusion.36), channel_id=1, source_target_pairs={{4,0},{8,4},{12,8},{16,12},{20,16},{24,20},{28,24},{32,28},{36,32}... | collective-permute-start | bytes 1152008 | tf_op jit(solution)/shard_map/ppermute | solution.py:14
  95.1 1.5 copy-start.5
  128.2 5.0 %copy-start.6 = (bf16[1,2,375,375]{3,1,2,0:T(2,128)(2,1)S(1)}, bf16[1,2,375,375]{3,1,2,0:T(2,128)(2,1)}, u32[]{:S(2)}) copy-start(bf16[1,2,375,375]{3,1,2,0:T(2,128)(2,1)} %param.12) | copy-start | bytes 1687504
Sparse Core Ops, SparseCore 0:
  96.8 31.4 all-gather.2
